TPU v7x, 256 devices: a whole 4x4x8 slice. The times are simulated.
256 devices in a mesh: ctx: 16 (over z, core), exp: 16 (over x, y).
Axes of the slice: x: 4, y: 4, z: 8, core: 2. Of those that a mesh axis runs over, the one named last changes fastest.
Arguments:
- inner_input: bfloat16 [8192, 8192], P('ctx', 'exp'), may hold values from -6 to 6
- gate_input: bfloat16 [8192, 8192], P('ctx', 'exp'), may hold values from -6 to 6
- coupling_input: bfloat16 [8192, 256], P('ctx'), may hold values from -6 to 6
- step_input: float32 [8192, 128], P('ctx', 'exp'), may hold values from -7 to 140
- conv_inner: float32 [4, 8192], P(None, 'exp'), may hold values from -3 to 3
- conv_coupling: float32 [4, 256], replicated, may hold values from -3 to 3
- decay_log: float32 [128], P('exp'), may hold values from -5.3 to -2.5
- skip_gain: float32 [128], P('exp'), may hold values from 0.5 to 2
- norm_gain: float32 [8192], P('exp'), may hold values from 0.1 to 1.9
- out_weight: bfloat16 [8192, 4096], P('exp'), may hold values from -0.0625 to 0.0625
- residual: bfloat16 [8192, 4096], P(('ctx', 'exp')), may hold values from -6 to 6
- moe_gain: float32 [4096], replicated, may hold values from 0.1 to 1.9
- router_weight: bfloat16 [4096, 72], replicated, may hold values from -0.1875 to 0.1875
- routes: int32 [8192, 10], P(('ctx', 'exp')), may hold values from 0 to 71, all different within a row
- priority: int32 [256, 32], P(('ctx', 'exp')), may hold values from 0 to 31, each once within a row
- expert_in: bfloat16 [16, 4096, 1536], P('exp', 'ctx'), may hold values from -0.09375 to 0.09375
- expert_out: bfloat16 [16, 4096, 768], P('exp', 'ctx'), may hold values from -0.21875 to 0.21875
Outputs:
- hidden: float32 [8192, 4096], P(('ctx', 'exp'))
- moe_out: float32 [8192, 4096], P(('ctx', 'exp'))
Inputs may be any that keep to these rules, and one draw needn't show every extreme that they name: `routes`: each token names 10 different experts. `priority`: the 32 tokens of each row carry distinct priorities.
All inputs are finite; a program needn't handle non-finite values.
Results may differ from a plain program's by a relative error of at most 0.029.
Values may be sent and summed in bfloat16 or wider, within the bound.
A program may use at most 128 MiB of HBM per device.

v0:
```python
import jax
import jax.numpy as jnp
from jax import lax
from jax.sharding import PartitionSpec as P

HDIM = 64
STATE = 128
KCONV = 4
NEXP = 72
TOPK = 10
FFE = 768
SPAN = 256
INNER = 8192
EPS = 1e-05
HIGH = lax.Precision.HIGHEST


def shifted(array, axis, by):
    devices = lax.axis_size(axis)
    pairs = [(i, i + by) for i in range(devices) if 0 <= i + by < devices]
    return lax.ppermute(array, axis, pairs)


def carried_in(part, axis, combine, identity):
    place = lax.axis_index(axis)
    gathered = jax.tree.map(lambda a: lax.all_gather(a, axis), part)
    state = jax.tree.map(lambda a, e: jnp.zeros_like(a) + jnp.asarray(e, a.dtype), part, identity)

    def one(step, state):
        return combine(
            state, jax.tree.map(lambda a: lax.dynamic_index_in_dim(a, step, 0, False), gathered)
        )

    return lax.fori_loop(0, place, one, state)


def causal_conv(values, before, weight):
    count = values.shape[0]
    padded = jnp.concatenate([before.astype(jnp.float32), values.astype(jnp.float32)], axis=0)
    total = jnp.zeros((count, values.shape[1]), jnp.float32)
    for k in range(KCONV):
        total = total + weight[k][None, :] * padded[k : k + count]
    return jax.nn.silu(total).astype(jnp.bfloat16)


def join_states(earlier, later):
    return (earlier[0] * later[0], later[0][:, None, None] * earlier[1] + later[1])


def body(
    inner_input,
    gate_input,
    coupling_input,
    step_input,
    conv_inner,
    conv_coupling,
    decay_log,
    skip_gain,
    norm_gain,
    out_weight,
    residual,
    moe_gain,
    router_weight,
    routes,
    priority,
    expert_in,
    expert_out,
):
    width = inner_input.shape[1]
    heads = decay_log.shape[0]
    count = inner_input.shape[0]
    blocks = count // SPAN
    edges = jnp.concatenate(
        [inner_input[count - (KCONV - 1) :], coupling_input[count - (KCONV - 1) :]], axis=1
    )
    before = shifted(edges, "ctx", 1)
    inner = causal_conv(inner_input, before[:, :width], conv_inner)
    coupling = causal_conv(coupling_input, before[:, width:], conv_coupling)
    steps = jax.nn.softplus(step_input).reshape(blocks, SPAN, heads)
    inner_parts = inner.reshape(blocks, SPAN, heads, HDIM)
    input_parts = coupling[:, :STATE].reshape(blocks, SPAN, STATE)
    output_parts = coupling[:, STATE:].reshape(blocks, SPAN, STATE)
    rate = steps * (-jnp.exp(decay_log))[None, None, :]
    cums = jnp.cumsum(rate, axis=1)
    scores = jnp.einsum(
        "cin,cjn->cij", output_parts, input_parts, preferred_element_type=jnp.float32
    )
    above = (jnp.arange(SPAN)[:, None] >= jnp.arange(SPAN)[None, :])[None, None]
    flipped = jnp.swapaxes(cums, 1, 2)
    spread = flipped[:, :, :, None] - flipped[:, :, None, :]
    decay = jnp.where(above, jnp.exp(jnp.where(above, spread, 0.0)), 0.0)
    mixing = (scores[:, None] * decay * jnp.swapaxes(steps, 1, 2)[:, :, None, :]).astype(
        jnp.bfloat16
    )
    local = jnp.einsum("chij,cjhp->cihp", mixing, inner_parts, preferred_element_type=jnp.float32)
    inner_wide = inner_parts.astype(jnp.float32)
    tail = jnp.exp(cums[:, -1:, :] - cums) * steps
    states = jnp.einsum(
        "cjh,cjn,cjhp->chnp", tail, input_parts.astype(jnp.float32), inner_wide, precision=HIGH
    )
    drops = jnp.exp(cums[:, -1, :])
    running = jnp.zeros((heads, STATE, HDIM), jnp.float32)
    reach = jnp.ones((heads,), jnp.float32)
    starts = []
    reaches = []
    for k in range(blocks):
        starts.append(running)
        reaches.append(reach)
        running = drops[k][:, None, None] * running + states[k]
        reach = reach * drops[k]
    neutral = (jnp.ones((heads,), jnp.float32), jnp.zeros((heads, STATE, HDIM), jnp.float32))
    incoming = carried_in((reach, running), "ctx", join_states, neutral)[1]
    entry = jnp.stack([reaches[k][:, None, None] * incoming + starts[k] for k in range(blocks)])
    carried = jnp.einsum(
        "cin,cih,chnp->cihp", output_parts.astype(jnp.float32), jnp.exp(cums), entry, precision=HIGH
    )
    mixed = (local + carried + skip_gain[None, None, :, None] * inner_wide).reshape(count, width)
    gated = mixed * jax.nn.silu(gate_input.astype(jnp.float32))
    squares = jnp.sum(gated * gated, axis=1)
    scaled = (gated * norm_gain[None, :]).astype(jnp.bfloat16)
    projected = jnp.dot(scaled, out_weight, preferred_element_type=jnp.float32)
    owned = lax.psum_scatter(
        projected.astype(jnp.bfloat16), "exp", scatter_dimension=0, tiled=True
    ).astype(jnp.float32)
    owned_squares = lax.psum_scatter(squares, "exp", scatter_dimension=0, tiled=True)
    mamba_out = owned * lax.rsqrt(owned_squares / INNER + EPS)[:, None]
    hidden = residual.astype(jnp.float32) + mamba_out
    tokens = hidden.shape[0]
    flight = lax.axis_size("exp")
    capacity = max(2, 2 * tokens * TOPK // NEXP)
    normed = (
        hidden * lax.rsqrt(jnp.mean(hidden * hidden, axis=1) + EPS)[:, None] * moe_gain[None, :]
    ).astype(jnp.bfloat16)
    logits = jnp.dot(normed, router_weight, preferred_element_type=jnp.float32)
    table = routes[:, :, None] == jnp.arange(NEXP, dtype=jnp.int32)[None, None, :]
    picked = jnp.sum(jnp.where(table, logits[:, None, :], 0.0), axis=2)
    raised = jnp.exp(picked)
    probs = raised / jnp.sum(raised, axis=1, keepdims=True)
    match = routes[:, :, None] == jnp.arange(flight, dtype=jnp.int32)[None, None, :]
    member = jnp.sum(match.astype(jnp.int32), axis=1)
    share = jnp.sum(jnp.where(match, probs[:, :, None], 0.0), axis=1).astype(jnp.bfloat16)
    order = priority[0]
    earlier = (order[None, :] < order[:, None]).astype(jnp.int32)
    rank = jnp.sum(earlier[:, :, None] * member[None, :, :], axis=1)
    kept = (member > 0) & (rank < capacity)
    slots = kept[:, :, None] & (
        rank[:, :, None] == jnp.arange(capacity, dtype=jnp.int32)[None, None, :]
    )
    select = jnp.transpose(slots, (1, 2, 0)).astype(jnp.bfloat16)
    outbound = jnp.einsum("fst,td->fsd", select, normed, preferred_element_type=jnp.float32).astype(
        jnp.bfloat16
    )
    arrived = lax.all_to_all(outbound, "exp", split_axis=0, concat_axis=0, tiled=True)
    rows = arrived.reshape(flight * capacity, normed.shape[1])
    slices = lax.axis_size("ctx")
    whole_in = lax.all_gather(expert_in[0], "ctx", axis=0, tiled=True)
    slice_width = rows.shape[1] // slices
    parts = jnp.einsum(
        "rkw,kwf->krf",
        rows.reshape(rows.shape[0], slices, slice_width),
        whole_in.reshape(slices, slice_width, 2 * FFE),
        preferred_element_type=jnp.float32,
    ).astype(jnp.bfloat16)
    units = jnp.sum(lax.optimization_barrier(parts).astype(jnp.float32), axis=0)
    activated = (jax.nn.silu(units[:, :FFE]) * units[:, FFE:]).astype(jnp.bfloat16)
    answer = jnp.einsum(
        "rf,df->rd",
        activated,
        lax.all_gather(expert_out[0], "ctx", axis=0, tiled=True),
        preferred_element_type=jnp.float32,
    ).astype(jnp.bfloat16)
    returned = lax.all_to_all(
        answer.reshape(flight, capacity, answer.shape[1]),
        "exp",
        split_axis=0,
        concat_axis=0,
        tiled=True,
    )
    weights = select * jnp.transpose(share)[:, None, :]
    moe_out = jnp.einsum("fst,fsd->td", weights, returned, preferred_element_type=jnp.float32)
    return (hidden, moe_out)


def solution(mesh):
    placed = (
        P("ctx", "exp"),
        P("ctx", "exp"),
        P("ctx", None),
        P("ctx", "exp"),
        P(None, "exp"),
        P(),
        P("exp"),
        P("exp"),
        P("exp"),
        P("exp", None),
        P(("ctx", "exp"), None),
        P(),
        P(),
        P(("ctx", "exp"), None),
        P(("ctx", "exp"), None),
        P("exp", "ctx", None),
        P("exp", "ctx", None),
    )
    return jax.shard_map(
        body,
        mesh=mesh,
        in_specs=placed,
        out_specs=(P(("ctx", "exp"), None), P(("ctx", "exp"), None)),
        check_vma=False,
    )
```

profile of v0, /device:TPU:32, one launch (start us, length us, event | category | flops | bytes accessed | tf_op | source)
XLA Modules:
  0.0 354.1 jit_solution(14720117451480724429)
XLA Ops:
  7.2 0.8 slice.91
  8.0 0.7 slice.92
  8.7 0.8 copy.91
  9.5 1.9 collective-permute-start
  11.4 0.7 compare_select_fusion
  12.2 0.7 exponential_negate_fusion
  12.9 1.1 reduce-window.6
  14.0 0.2 slice_reduce_fusion
  14.3 0.7 fusion.63
  14.9 0.2 slice_reduce_fusion.1
  15.2 0.8 fusion.66
  16.0 0.9 fusion.65
  16.9 0.6 slice_bitcast_fusion.1
  17.5 1.0 convert_element_type.80
  18.5 1.3 copy.92
  19.7 0.1 convert_element_type.77
  19.9 0.1 copy.93
  20.0 0.3 multiply_convert_fusion.12
  20.4 1.5 multiply_convert_fusion.9
  21.9 0.1 reshape.148
  22.0 0.7 convolution_bitcast_fusion.1
  22.7 0.8 slice_add_fusion
  23.6 0.2 copy.102
  23.8 19.0 %all-gather.2 = f32[16,1,8]{2,1,0:T(1,128)} all-gather(f32[1,1,8]{2,1,0:T(1,128)S(1)} %get-tuple-element.98), channel_id=1, replica_groups=mesh['ctx'=16,'exp'=16] {'ctx'}, dimensions={0}, use_global_device_ids=true | all-gather | bytes 544 | tf_op jit(solution)/shard_map/all_gather | solution.py:26
  42.9 0.7 add_bitcast_fusion.1
  43.5 1.0 fusion.67
  44.6 24.1 %all-gather.7.cloned.1.call-done = f32[16,8,128,64]{2,3,1,0:T(8,128)} async-done(((f32[1,8,128,64]{2,3,1,0:T(8,128)}), f32[16,8,128,64]{2,3,1,0:T(8,128)}) %all-gather.7.cloned.1.call-update) | async-done | bytes 4194320 | tf_op jit(solution)/shard_map/all_gather | solution.py:26
  68.7 4.1 %while.12 = (s32[]{:T(128)}, f32[8,128,64]{2,1,0:T(8,128)S(1)}, s32[]{:T(128)}, f32[16,8]{1,0:T(8,128)}, f32[16,8,128,64]{2,3,1,0:T(8,128)}, /*index=5*/s32[]{:T(128)}, s32[]{:T(128)}, s32[]{:T(128)}) while((s32[]{:T(128)}, f32[8,128,64]{2,1,0:T(8,128)S(1)}, s32[]{:T(128)}, f32[16,8]{1,0:T(8,128)}, f32[16,8,128,64]{2,3,1,0:T(8,128)}, ...), condition=%wide.region_3.4_spmd, body=%wide.region_2.3_spmd.sunk | while | flops 131077 | bytes 1835231 | solution.py:34
  68.8 1.0 constant_dynamic-slice_fusion.2
  69.7 0.2 copy.125
  69.9 0.7 dynamic-slice_bitcast_fusion.2
  70.6 0.1 bitcast_add_fusion.3
  70.8 1.0 constant_dynamic-slice_fusion.2
  71.8 0.2 copy.125
  72.0 0.7 dynamic-slice_bitcast_fusion.2
  72.7 0.1 bitcast_add_fusion.3
  72.9 0.2 copy.99
  73.0 0.8 fusion.47
  73.9 1.5 fusion.68
  75.4 2.3 fusion.17
  77.7 0.8 copy.101
  78.6 1.3 copy-done.10
  79.9 4.6 %convolution_convert_fusion = bf16[512,4096]{1,0:T(8,128)(2,1)} fusion(bf16[512,4096]{1,0:T(8,128)(2,1)S(1)} %copy-done.10, f32[512]{0:T(512)S(1)} %copy-done.11, f32[512,512]{0,1:T(8,128)S(1)} %bitcast.109, bf16[512,512]{0,1:T(8,128)(2,1)S(1)} %copy.102), kind=kOutput, calls=%fused_computation.6 | convolution fusion | flops 2151677952 | bytes 9963520 | tf_op jit(solution)/shard_map/dot_general | solution.py:121
  84.6 0.7 all-gather.9.cloned.1.call-update
  85.4 0.5 all-gather.11.cloned.1.call-update
  86.0 0.6 multiply_reduce_fusion.2
  86.7 0.6 dynamic-slice
  88.0 0.4 multiply_reduce_fusion
  88.4 40.4 %all-reduce = f32[512]{0:T(512)S(1)} all-reduce(f32[512]{0:T(512)S(1)} %multiply_reduce_fusion), channel_id=5, replica_groups=mesh['ctx'=16,'exp'=16] {'exp'}, use_global_device_ids=true, to_apply=%region_6.7.clone | all-reduce | flops 512 | bytes 4096
  128.9 63.8 %reduce-scatter.2.cloned.1.call-done = bf16[32,4096]{1,0:T(8,128)(2,1)} async-done(((bf16[512,4096]{1,0:T(8,128)(2,1)}), bf16[32,4096]{1,0:T(8,128)(2,1)}) %reduce-scatter.2.cloned.1.call-update) | async-done | bytes 262160 | tf_op jit(solution)/shard_map/reduce_scatter | solution.py:122
  192.6 1.2 multiply_reduce_fusion.1
  193.9 0.5 convolution_convert_fusion.2
  194.4 19.8 %all_to_all.10 = bf16[16,8,4096]{2,1,0:T(8,128)(2,1)S(1)} all-to-all(bf16[16,8,4096]{2,1,0:T(8,128)(2,1)S(1)} %convolution_convert_fusion.2), channel_id=1, replica_groups=mesh['ctx'=16,'exp'=16] {'exp'}, dimensions={0} | all-to-all | bytes 2097152 | tf_op jit(solution)/shard_map/all_to_all | solution.py:153
  214.2 0.2 copy.111
  214.5 53.0 %all-gather.9.cloned.1.call-done = bf16[1,4096,1536]{2,1,0:T(8,128)(2,1)} async-done(((bf16[1,256,1536]{2,1,0:T(8,128)(2,1)}), bf16[1,4096,1536]{2,1,0:T(8,128)(2,1)}) %all-gather.9.cloned.1.call-update) | async-done | bytes 12582928 | tf_op jit(solution)/shard_map/all_gather | solution.py:156
  267.5 6.6 %convolution_convert_fusion.1 = bf16[16,128,1536]{2,1,0:T(8,128)(2,1)S(1)} fusion(bf16[16,256,1536]{2,1,0:T(8,128)(2,1)} %bitcast.107, bf16[128,16,256]{2,1,0:T(8,128)(2,1)S(1)} %bitcast.108), kind=kOutput, calls=%fused_computation.7 | convolution fusion | flops 1613758464 | bytes 19922944 | tf_op jit(solution)/shard_map/rkw,kwf->krf/dot_general | solution.py:158
  274.1 0.9 convert_reduce_fusion
  275.0 40.1 %all-gather.11.cloned.1.call-done = bf16[1,4096,768]{2,1,0:T(8,128)(2,1)} async-done(((bf16[1,256,768]{2,1,0:T(8,128)(2,1)}), bf16[1,4096,768]{2,1,0:T(8,128)(2,1)}) %all-gather.11.cloned.1.call-update) | async-done | bytes 6291472 | tf_op jit(solution)/shard_map/all_gather | solution.py:169
  315.1 5.9 %fusion.5 = bf16[16,8,4096]{2,1,0:T(8,128)(2,1)} fusion(bf16[1,4096,768]{2,1,0:T(8,128)(2,1)} %all-gather.11.cloned.1.call-done, f32[128,1536]{1,0:T(8,128)S(1)} %convert_reduce_fusion), kind=kOutput, calls=%fused_computation.10 | convolution fusion | flops 806420480 | bytes 8126464 | tf_op jit(solution)/shard_map/rf,df->rd/dot_general | solution.py:166
  321.0 6.8 %all-to-all-start.1 = ((bf16[16,8,4096]{2,1,0:T(8,128)(2,1)}), bf16[16,8,4096]{2,1,0:T(8,128)(2,1)S(1)}, u32[]{:S(2)}, u32[]{:S(2)}) async-start(bf16[16,8,4096]{2,1,0:T(8,128)(2,1)} %fusion.5), calls=%async_computation.2 | async-start | bytes 2097152 | tf_op jit(solution)/shard_map/all_to_all | solution.py:172
  327.8 0.4 fusion.61
  328.1 0.2 select_reduce_fusion
  328.4 17.6 %all-to-all-done.1 = bf16[16,8,4096]{2,1,0:T(8,128)(2,1)S(1)} async-done(((bf16[16,8,4096]{2,1,0:T(8,128)(2,1)}), bf16[16,8,4096]{2,1,0:T(8,128)(2,1)S(1)}, u32[]{:S(2)}, u32[]{:S(2)}) %all-to-all-start.1) | async-done | bytes 1048608 | tf_op jit(solution)/shard_map/all_to_all | solution.py:172
  346.0 1.5 convolution_bitcast_fusion
  (57 shorter events, 1.0 us)
Async XLA Ops:
  7.2 320.6 %copy-start = (bf16[4096,72]{0,1:T(8,128)(2,1)S(1)}, bf16[4096,72]{0,1:T(8,128)(2,1)}, u32[]{:S(2)}) copy-start(bf16[4096,72]{0,1:T(8,128)(2,1)} %param.31) | copy-start | bytes 1769476
  7.2 61.5 %all-gather.7.cloned.1.call-start = ((), (), s32[]{:S(2)}) async-start(), calls=%async_computation.3 | async-start | bytes 4456448 | tf_op jit(solution)/shard_map/all_gather | solution.py:26
  9.5 10.3 %collective-permute-start = (bf16[3,768]{0,1:T(8,128)(2,1)}, bf16[3,768]{0,1:T(8,128)(2,1)S(1)}, u32[]{:S(2)}, u32[]{:S(2)}) collective-permute-start(bf16[3,768]{0,1:T(8,128)(2,1)} %copy.91), channel_id=1, source_target_pairs={{0,16},{16,32},{32,48},{48,64},{64,80},{80,96},{96,112},{112,128},... | collective-permute-start | bytes 13832 | tf_op jit(solution)/shard_map/ppermute | solution.py:21
  17.5 5.2 %copy-start.8 = (f32[8]{0:T(128)}, f32[8]{0:T(128)S(1)}, u32[]{:S(2)}) copy-start(f32[8]{0:T(128)S(1)} %broadcast_multiply_fusion) | copy-start | bytes 100
  19.7 3.9 %copy-start.4 = (bf16[512,512]{1,0:T(8,128)(2,1)S(1)}, bf16[512,512]{1,0:T(8,128)(2,1)}, u32[]{:S(2)}) copy-start(bf16[512,512]{1,0:T(8,128)(2,1)} %param.20) | copy-start | bytes 1572868
  20.4 48.3 %copy-start.2 = (bf16[512,128]{1,0:T(8,128)(2,1)}, bf16[512,128]{1,0:T(8,128)(2,1)S(1)}, u32[]{:S(2)}) copy-start(bf16[512,128]{1,0:T(8,128)(2,1)S(1)} %get-tuple-element.87) | copy-start | bytes 393220
  23.5 169.1 %reduce-scatter.2.cloned.1.call-start = ((), (), s32[]{:S(2)}) async-start(), calls=%async_computation.4 | async-start | bytes 4456448 | tf_op jit(solution)/shard_map/reduce_scatter | solution.py:122
  72.8 2.5 copy-start.3
  77.7 2.2 copy-start.10
  77.7 2.2 copy-start.11
  84.5 1.4 copy-start.6
  84.5 1.4 copy-start.9
  84.5 2.2 copy-start.12
  84.5 108.1 %copy-start.5 = (bf16[32,4096]{1,0:T(8,128)(2,1)S(1)}, bf16[32,4096]{1,0:T(8,128)(2,1)}, u32[]{:S(2)}) copy-start(bf16[32,4096]{1,0:T(8,128)(2,1)} %param.29) | copy-start | bytes 786436
  84.6 109.3 %copy-start.7 = (f32[4096]{0:T(1024)S(1)}, f32[4096]{0:T(1024)}, u32[]{:S(2)}) copy-start(f32[4096]{0:T(1024)} %param.30) | copy-start | bytes 49156
  84.6 182.9 %all-gather.9.cloned.1.call-start = ((), (), s32[]{:S(2)}) async-start(), calls=%async_computation.5 | async-start | bytes 13369344 | tf_op jit(solution)/shard_map/all_gather | solution.py:156
  85.3 229.7 %all-gather.11.cloned.1.call-start = ((), (), s32[]{:S(2)}) async-start(), calls=%async_computation.6 | async-start | bytes 6684672 | tf_op jit(solution)/shard_map/all_gather | solution.py:169
  193.9 133.9 %copy-start.1 = (f32[32,4096]{1,0:T(8,128)}, f32[32,4096]{1,0:T(8,128)S(1)}, u32[]{:S(2)}) copy-start(f32[32,4096]{1,0:T(8,128)S(1)} %get-tuple-element.83) | copy-start | bytes 1572868
  321.0 25.0 %all-to-all-start.1 = ((bf16[16,8,4096]{2,1,0:T(8,128)(2,1)}), bf16[16,8,4096]{2,1,0:T(8,128)(2,1)S(1)}, u32[]{:S(2)}, u32[]{:S(2)}) async-start(bf16[16,8,4096]{2,1,0:T(8,128)(2,1)} %fusion.5), calls=%async_computation.2 | async-start | bytes 2097152 | tf_op jit(solution)/shard_map/all_to_all | solution.py:172
Sparse Core Ops, SparseCore 0:
  23.6 44.9 all-gather.6
  84.7 107.8 reduce-scatter.1
  194.5 72.9 all-gather.8
  269.2 45.8 all-gather.10
where the time goes:
time: 356 us; the launch traced here: 354 us
  waiting for transfers between devices  200 us (56%)
  blocking collectives  79.3 us (22%)
  matrix products  25.1 us (7%)
  between operations  14.8 us (4%)
  local copies, waits for them, and re-layouts  13.1 us (4%)
  other arithmetic  13.1 us (4%)
  starting transfers between devices  8.84 us (2%)
    reduce_scatter x1, waiting for transfers between devices, body(): lax.psum_scatter(projected.astype(jnp.bfloat16), 'exp', scatter_dimension...  63.8 us
    all_gather x1, waiting for transfers between devices, body(): whole_in = lax.all_gather(expert_in[0], 'ctx', axis=0, tiled=True)  53 us
    unnamed x1, blocking collectives  40.4 us
    all_gather x1, waiting for transfers between devices, body(): lax.all_gather(expert_out[0], 'ctx', axis=0, tiled=True)  40.1 us
    all_gather x1, waiting for transfers between devices, carried_in(): gathered = jax.tree.map(lambda a: lax.all_gather(a, axis), part)  24.1 us
    all_to_all x1, blocking collectives, body(): lax.all_to_all(outbound, 'exp', split_axis=0, concat_axis=0, tiled=True)  19.8 us
    all_gather x1, blocking collectives, carried_in(): gathered = jax.tree.map(lambda a: lax.all_gather(a, axis), part)  19 us
    all_to_all x1, waiting for transfers between devices, body(): lax.all_to_all(answer.reshape(flight, capacity, answer.shape[1]), 'exp',...  17.6 us
  transfers between devices with their start and end apart: 6, of which 5 were waited for; matrix products, arithmetic and copies ran while one was open for 6% of the time, Pallas kernels for 0%

commit v1 on v0

--- a/solution.py
+++ b/solution.py
@@ -13,6 +13,28 @@
 INNER = 8192
 EPS = 1e-05
 HIGH = lax.Precision.HIGHEST
+
+
+def joined_along(blocks, dim):
+    blocks = jnp.moveaxis(blocks, 0, dim)
+    lengths = blocks.shape
+    return blocks.reshape(*lengths[:dim], lengths[dim] * lengths[dim + 1], *lengths[dim + 2 :])
+
+
+def ring_gather(shard, axis, dim):
+    size = lax.axis_size(axis)
+    pairs = [(i, (i + 1) % size) for i in range(size)]
+    back = [(b, a) for a, b in pairs]
+    lower, upper = ([], [])
+    for step in range(size - 1):
+        if step % 2 == 0:
+            lower.append(lax.ppermute(lower[-1] if lower else shard, axis, pairs))
+        else:
+            upper.append(lax.ppermute(upper[-1] if upper else shard, axis, back))
+    blocks = jnp.stack([*lower[::-1], shard, *upper])
+    shift = lax.axis_index(axis) - len(lower)
+    blocks = blocks[(jnp.arange(size) - shift) % size]
+    return joined_along(blocks, dim)
 
 
 def shifted(array, axis, by):
@@ -166,7 +188,7 @@
     answer = jnp.einsum(
         "rf,df->rd",
         activated,
-        lax.all_gather(expert_out[0], "ctx", axis=0, tiled=True),
+        ring_gather(expert_out[0], "ctx", 0),
         preferred_element_type=jnp.float32,
     ).astype(jnp.bfloat16)
     returned = lax.all_to_all(

time: 356 us -> 305 us (0.86)
  waiting for transfers between devices: 200 us -> 99.3 us
  starting transfers between devices: 8.84 us -> 45 us
  local copies, waits for them, and re-layouts: 13.1 us -> 45.1 us
  blocking collectives: 79.3 us -> 58.8 us
    reduce_scatter x1, waiting for transfers between devices: 63.8 us -> 0.01 us  [body(): lax.psum_scatter(projected.astype(jnp.bfloat16), 'exp', scatter_dimension...]
    ppermute x0 -> x15, waiting for transfers between devices: none -> 41.3 us  [the longest x8 39.5 us: ring_gather(): lower.append(lax.ppermute(lower[-1] if lower else shard, axis, pairs))]
    all_gather x1 -> x0, waiting for transfers between devices: 40.1 us -> none  [body(): lax.all_gather(expert_out[0], 'ctx', axis=0, tiled=True)]
    all_gather x1, waiting for transfers between devices: 53 us -> 16.7 us  [body(): whole_in = lax.all_gather(expert_in[0], 'ctx', axis=0, tiled=True)]
    ppermute x0 -> x15, starting transfers between devices: none -> 31.8 us  [the longest x7 28.5 us: ring_gather(): upper.append(lax.ppermute(upper[-1] if upper else shard, axis, back))]
    unnamed x31 -> x68, local copies, waits for them, and re-layouts: 3.72 us -> 28.3 us
    all_to_all x1 -> x0, blocking collectives: 19.8 us -> none  [body(): lax.all_to_all(outbound, 'exp', split_axis=0, concat_axis=0, tiled=True)]
    gather x0 -> x1, local copies, waits for them, and re-layouts: none -> 6.46 us  [ring_gather(): blocks = blocks[(jnp.arange(size) - shift) % size]]
  transfers between devices with their start and end apart: 6 -> 21, of which waited for: 5 -> 12; matrix products, arithmetic and copies ran while one was open for 6% -> 17% of each run, Pallas kernels for 0% -> 0%
where the time goes in v1:
time: 305 us; the launch traced here: 302 us
  waiting for transfers between devices  99.3 us (33%)
  blocking collectives  58.8 us (19%)
  local copies, waits for them, and re-layouts  45.1 us (15%)
  starting transfers between devices  45 us (15%)
  matrix products  25 us (8%)
  between operations  14.9 us (5%)
  other arithmetic  13.8 us (5%)
    unnamed x1, blocking collectives  40.7 us
    ppermute x8, waiting for transfers between devices, ring_gather(): lower.append(lax.ppermute(lower[-1] if lower else shard, axis, pairs))  39.5 us
    ppermute x7, starting transfers between devices, ring_gather(): upper.append(lax.ppermute(upper[-1] if upper else shard, axis, back))  28.5 us
    unnamed x68, local copies, waits for them, and re-layouts  28.3 us
    all_gather x1, waiting for transfers between devices, carried_in(): gathered = jax.tree.map(lambda a: lax.all_gather(a, axis), part)  23 us
    all_gather x1, blocking collectives, carried_in(): gathered = jax.tree.map(lambda a: lax.all_gather(a, axis), part)  18.1 us
    all_to_all x1, waiting for transfers between devices, body(): lax.all_to_all(answer.reshape(flight, capacity, answer.shape[1]), 'exp',...  17.6 us
    all_gather x1, waiting for transfers between devices, body(): whole_in = lax.all_gather(expert_in[0], 'ctx', axis=0, tiled=True)  16.7 us
  transfers between devices with their start and end apart: 21, of which 12 were waited for; matrix products, arithmetic and copies ran while one was open for 17% of the time, Pallas kernels for 0%

profile of v1, /device:TPU:32, one launch (start us, length us, event | category | flops | bytes accessed | tf_op | source)
XLA Modules:
  0.0 302.0 jit_solution(6567205525784470750)
XLA Ops:
  8.9 1.9 collective-permute-start
  12.3 1.1 reduce-window.6
  13.9 0.8 fusion.61
  14.8 1.4 fusion.60
  17.3 1.0 convert_element_type.80
  18.3 1.3 copy.92
  20.8 2.2 multiply_convert_fusion.9
  23.9 1.4 slice_add_fusion
  25.4 1.3 copy.102
  26.7 18.1 %all-gather.1 = f32[16,1,8]{2,1,0:T(1,128)S(1)} all-gather(f32[1,1,8]{2,1,0:T(1,128)} %get-tuple-element.98), channel_id=1, replica_groups=mesh['ctx'=16,'exp'=16] {'ctx'}, dimensions={0}, use_global_device_ids=true | all-gather | bytes 544 | tf_op jit(solution)/shard_map/all_gather | solution.py:48
  45.5 2.0 fusion.62
  47.5 23.0 %all-gather.5.cloned.1.call-done = f32[16,8,128,64]{2,3,1,0:T(8,128)} async-done(((f32[1,8,128,64]{2,3,1,0:T(8,128)}), f32[16,8,128,64]{2,3,1,0:T(8,128)}) %all-gather.5.cloned.1.call-update) | async-done | bytes 4194320 | tf_op jit(solution)/shard_map/all_gather | solution.py:48
  70.6 2.8 while.12
  70.6 1.0 constant_dynamic-slice_fusion.2
  72.0 1.0 constant_dynamic-slice_fusion.2
  73.7 1.5 fusion.63
  75.2 2.7 fusion.10
  78.0 0.8 copy.101
  78.9 4.5 %convolution_convert_fusion = bf16[512,4096]{1,0:T(8,128)(2,1)} fusion(bf16[512,4096]{1,0:T(8,128)(2,1)S(1)} %copy-done.18, f32[512]{0:T(512)S(1)} %copy-done.19, f32[512,512]{0,1:T(8,128)S(1)} %bitcast.140, bf16[512,512]{0,1:T(8,128)(2,1)S(1)} %copy.102), kind=kOutput, calls=%fused_computation.5 | convolution fusion | flops 2151677952 | bytes 9963520 | tf_op jit(solution)/shard_map/dot_general | solution.py:143
  84.2 1.6 collective-permute-start.1
  85.9 5.6 %collective-permute-done.1 = bf16[256,768]{1,0:T(8,128)(2,1)S(1)} collective-permute-done((bf16[256,768]{1,0:T(8,128)(2,1)S(1)}, bf16[256,768]{1,0:T(8,128)(2,1)S(1)}, u32[]{:S(2)}, u32[]{:S(2)}) %collective-permute-start.1) | collective-permute-done | bytes 393248 | tf_op jit(solution)/shard_map/ppermute | solution.py:31
  91.5 0.8 collective-permute-start.2
  92.3 0.9 collective-permute-start.9
  93.2 5.5 %collective-permute-done.2 = bf16[256,768]{1,0:T(8,128)(2,1)S(1)} collective-permute-done((bf16[256,768]{1,0:T(8,128)(2,1)S(1)}, bf16[256,768]{1,0:T(8,128)(2,1)S(1)}, u32[]{:S(2)}, u32[]{:S(2)}) %collective-permute-start.2) | collective-permute-done | bytes 393248 | tf_op jit(solution)/shard_map/ppermute | solution.py:31
  98.7 0.8 collective-permute-start.3
  99.5 12.2 %collective-permute-start.10 = (bf16[256,768]{1,0:T(8,128)(2,1)S(1)}, bf16[256,768]{1,0:T(8,128)(2,1)S(1)}, u32[]{:S(2)}, u32[]{:S(2)}) collective-permute-start(bf16[256,768]{1,0:T(8,128)(2,1)S(1)} %collective-permute-done.9), channel_id=1, source_target_pairs={{16,0},{32,16},{48,32},{64,48},{80,64},{96,80},{112,96},{128,112},... | collective-permute-start | bytes 1179656 | tf_op jit(solution)/shard_map/ppermute | solution.py:33
  111.7 5.3 %collective-permute-done.3 = bf16[256,768]{1,0:T(8,128)(2,1)S(1)} collective-permute-done((bf16[256,768]{1,0:T(8,128)(2,1)S(1)}, bf16[256,768]{1,0:T(8,128)(2,1)S(1)}, u32[]{:S(2)}, u32[]{:S(2)}) %collective-permute-start.3) | collective-permute-done | bytes 393248 | tf_op jit(solution)/shard_map/ppermute | solution.py:31
  117.1 3.1 %collective-permute-start.11 = (bf16[256,768]{1,0:T(8,128)(2,1)S(1)}, bf16[256,768]{1,0:T(8,128)(2,1)S(1)}, u32[]{:S(2)}, u32[]{:S(2)}) collective-permute-start(bf16[256,768]{1,0:T(8,128)(2,1)S(1)} %collective-permute-done.10), channel_id=1, source_target_pairs={{16,0},{32,16},{48,32},{64,48},{80,64},{96,80},{112,96},{128,112},... | collective-permute-start | bytes 1179656 | tf_op jit(solution)/shard_map/ppermute | solution.py:33
  120.2 5.3 %collective-permute-done.4 = bf16[256,768]{1,0:T(8,128)(2,1)S(1)} collective-permute-done((bf16[256,768]{1,0:T(8,128)(2,1)S(1)}, bf16[256,768]{1,0:T(8,128)(2,1)S(1)}, u32[]{:S(2)}, u32[]{:S(2)}) %collective-permute-start.4) | collective-permute-done | bytes 393248 | tf_op jit(solution)/shard_map/ppermute | solution.py:31
  125.5 3.1 %collective-permute-start.12 = (bf16[256,768]{1,0:T(8,128)(2,1)S(1)}, bf16[256,768]{1,0:T(8,128)(2,1)}, u32[]{:S(2)}, u32[]{:S(2)}) collective-permute-start(bf16[256,768]{1,0:T(8,128)(2,1)S(1)} %collective-permute-done.11), channel_id=1, source_target_pairs={{16,0},{32,16},{48,32},{64,48},{80,64},{96,80},{112,96},{128,112},... | collective-permute-start | bytes 1179656 | tf_op jit(solution)/shard_map/ppermute | solution.py:33
  128.6 5.3 %collective-permute-done.5 = bf16[256,768]{1,0:T(8,128)(2,1)S(1)} collective-permute-done((bf16[256,768]{1,0:T(8,128)(2,1)S(1)}, bf16[256,768]{1,0:T(8,128)(2,1)S(1)}, u32[]{:S(2)}, u32[]{:S(2)}) %collective-permute-start.5) | collective-permute-done | bytes 393248 | tf_op jit(solution)/shard_map/ppermute | solution.py:31
  134.6 3.0 collective-permute-start.13
  137.6 4.8 %collective-permute-done.6 = bf16[256,768]{1,0:T(8,128)(2,1)} collective-permute-done((bf16[256,768]{1,0:T(8,128)(2,1)S(1)}, bf16[256,768]{1,0:T(8,128)(2,1)}, u32[]{:S(2)}, u32[]{:S(2)}) %collective-permute-start.6) | collective-permute-done | bytes 393248 | tf_op jit(solution)/shard_map/ppermute | solution.py:31
  144.4 3.0 collective-permute-start.14
  147.4 3.8 %collective-permute-done.7 = bf16[256,768]{1,0:T(8,128)(2,1)} collective-permute-done((bf16[256,768]{1,0:T(8,128)(2,1)}, bf16[256,768]{1,0:T(8,128)(2,1)}, u32[]{:S(2)}, u32[]{:S(2)}) %collective-permute-start.7) | collective-permute-done | bytes 393248 | tf_op jit(solution)/shard_map/ppermute | solution.py:31
  151.2 1.8 collective-permute-done.14
  153.0 3.3 %collective-permute-start.15 = (bf16[256,768]{1,0:T(8,128)(2,1)}, bf16[256,768]{1,0:T(8,128)(2,1)}, u32[]{:S(2)}, u32[]{:S(2)}) collective-permute-start(bf16[256,768]{1,0:T(8,128)(2,1)} %collective-permute-done.14), channel_id=1, source_target_pairs={{16,0},{32,16},{48,32},{64,48},{80,64},{96,80},{112,96},{128,112},... | collective-permute-start | bytes 1179656 | tf_op jit(solution)/shard_map/ppermute | solution.py:33
  156.3 4.0 %collective-permute-done.8 = bf16[256,768]{1,0:T(8,128)(2,1)S(1)} collective-permute-done((bf16[256,768]{1,0:T(8,128)(2,1)}, bf16[256,768]{1,0:T(8,128)(2,1)S(1)}, u32[]{:S(2)}, u32[]{:S(2)}) %collective-permute-start.8) | collective-permute-done | bytes 393248 | tf_op jit(solution)/shard_map/ppermute | solution.py:31
  160.2 0.8 bitcast_dynamic-update-slice_fusion.14
  161.0 1.8 bitcast_dynamic-update-slice_fusion.13
  162.8 1.8 bitcast_dynamic-update-slice_fusion.12
  164.6 1.8 bitcast_dynamic-update-slice_fusion.11
  166.3 1.8 bitcast_dynamic-update-slice_fusion.10
  168.1 1.8 bitcast_dynamic-update-slice_fusion.9
  169.9 1.8 bitcast_dynamic-update-slice_fusion.8
  172.5 0.8 constant_dynamic-update-slice_fusion
  175.2 40.7 %all-reduce = f32[512]{0:T(512)S(1)} all-reduce(f32[512]{0:T(512)S(1)} %multiply_reduce_fusion), channel_id=4, replica_groups=mesh['ctx'=16,'exp'=16] {'exp'}, use_global_device_ids=true, to_apply=%region_6.7.clone | all-reduce | flops 512 | bytes 4096
  216.0 1.3 multiply_reduce_fusion.1
  217.3 1.5 convolution_convert_fusion.3
  218.8 4.3 %all-to-all-start = ((bf16[16,8,4096]{2,1,0:T(8,128)(2,1)}), bf16[16,8,4096]{2,1,0:T(8,128)(2,1)}, u32[]{:S(2)}, u32[]{:S(2)}) async-start(bf16[16,8,4096]{2,1,0:T(8,128)(2,1)} %convolution_convert_fusion.3), calls=%async_computation.1 | async-start | bytes 2097152 | tf_op jit(solution)/shard_map/all_to_all | solution.py:175
  223.1 1.8 bitcast_dynamic-update-slice_fusion.4
  224.9 1.8 bitcast_dynamic-update-slice_fusion.3
  226.7 1.8 bitcast_dynamic-update-slice_fusion.2
  228.5 1.8 bitcast_dynamic-update-slice_fusion.1
  230.3 1.8 bitcast_dynamic-update-slice_fusion
  232.1 6.5 %gather_fusion = bf16[16,256,768]{2,1,0:T(8,128)(2,1)} fusion(bf16[16,256,768]{2,1,0:T(8,128)(2,1)} %bitcast_dynamic-update-slice_fusion, s32[1024]{0:T(1024)S(1)} %pad_clamp_fusion), kind=kCustom, calls=%fused_computation | custom fusion | bytes 12582976 | tf_op jit(solution)/shard_map/gather | solution.py:36
  238.5 2.6 copy.111
  241.2 16.7 %all-gather.7.cloned.1.call-done = bf16[1,4096,1536]{2,1,0:T(8,128)(2,1)} async-done(((bf16[1,256,1536]{2,1,0:T(8,128)(2,1)}), bf16[1,4096,1536]{2,1,0:T(8,128)(2,1)}) %all-gather.7.cloned.1.call-update) | async-done | bytes 12582928 | tf_op jit(solution)/shard_map/all_gather | solution.py:178
  257.8 7.1 %convolution_convert_fusion.1 = bf16[16,128,1536]{2,1,0:T(8,128)(2,1)S(1)} fusion(bf16[16,256,1536]{2,1,0:T(8,128)(2,1)} %bitcast.135, bf16[128,16,256]{2,1,0:T(8,128)(2,1)} %bitcast.139), kind=kOutput, calls=%fused_computation.6 | convolution fusion | flops 1613758464 | bytes 19922944 | tf_op jit(solution)/shard_map/rkw,kwf->krf/dot_general | solution.py:180
  264.9 0.9 convert_reduce_fusion
  265.8 3.1 %fusion = bf16[16,8,4096]{2,1,0:T(8,128)(2,1)} fusion(bf16[4096,768]{1,0:T(8,128)(2,1)S(1)} %bitcast.138, f32[128,1536]{1,0:T(8,128)S(1)} %convert_reduce_fusion), kind=kOutput, calls=%fused_computation.9 | convolution fusion | flops 806420480 | bytes 8126464 | tf_op jit(solution)/shard_map/rf,df->rd/dot_general | solution.py:188
  268.9 6.8 %all-to-all-start.1 = ((bf16[16,8,4096]{2,1,0:T(8,128)(2,1)}), bf16[16,8,4096]{2,1,0:T(8,128)(2,1)S(1)}, u32[]{:S(2)}, u32[]{:S(2)}) async-start(bf16[16,8,4096]{2,1,0:T(8,128)(2,1)} %fusion), calls=%async_computation.2 | async-start | bytes 2097152 | tf_op jit(solution)/shard_map/all_to_all | solution.py:194
  276.4 17.6 %all-to-all-done.1 = bf16[16,8,4096]{2,1,0:T(8,128)(2,1)S(1)} async-done(((bf16[16,8,4096]{2,1,0:T(8,128)(2,1)}), bf16[16,8,4096]{2,1,0:T(8,128)(2,1)S(1)}, u32[]{:S(2)}, u32[]{:S(2)}) %all-to-all-start.1) | async-done | bytes 1048608 | tf_op jit(solution)/shard_map/all_to_all | solution.py:194
  294.0 1.5 convolution_bitcast_fusion
  (127 shorter events, 15.1 us)
Async XLA Ops:
  7.2 268.6 %copy-start = (bf16[4096,72]{0,1:T(8,128)(2,1)S(1)}, bf16[4096,72]{0,1:T(8,128)(2,1)}, u32[]{:S(2)}) copy-start(bf16[4096,72]{0,1:T(8,128)(2,1)} %param.31) | copy-start | bytes 1769476
  7.2 63.3 %all-gather.5.cloned.1.call-start = ((), (), s32[]{:S(2)}) async-start(), calls=%async_computation.3 | async-start | bytes 4456448 | tf_op jit(solution)/shard_map/all_gather | solution.py:48
  8.9 10.8 %collective-permute-start = (bf16[3,768]{0,1:T(8,128)(2,1)S(1)}, bf16[3,768]{0,1:T(8,128)(2,1)S(1)}, u32[]{:S(2)}, u32[]{:S(2)}) collective-permute-start(bf16[3,768]{0,1:T(8,128)(2,1)S(1)} %copy.91), channel_id=1, source_target_pairs={{0,16},{16,32},{32,48},{48,64},{64,80},{80,96},{96,112},{112,128},... | collective-permute-start | bytes 13832 | tf_op jit(solution)/shard_map/ppermute | solution.py:43
  20.8 4.6 %copy-start.2 = (bf16[512,128]{1,0:T(8,128)(2,1)}, bf16[512,128]{1,0:T(8,128)(2,1)S(1)}, u32[]{:S(2)}) copy-start(bf16[512,128]{1,0:T(8,128)(2,1)S(1)} %get-tuple-element.86) | copy-start | bytes 393220
  25.3 190.6 %reduce-scatter.2.cloned.1.call-start = ((), (), s32[]{:S(2)}) async-start(), calls=%async_computation.4 | async-start | bytes 4456448 | tf_op jit(solution)/shard_map/reduce_scatter | solution.py:144
  70.5 3.0 copy-start.15
  70.5 3.0 copy-start.16
  70.5 4.6 %copy-start.20 = (f32[8]{0:T(128)S(1)}, f32[8]{0:T(128)}, u32[]{:S(2)}) copy-start(f32[8]{0:T(128)} %param.26) | copy-start | bytes 100
  75.2 3.7 %copy-start.18 = (bf16[512,4096]{1,0:T(8,128)(2,1)S(1)}, bf16[512,4096]{1,0:T(8,128)(2,1)}, u32[]{:S(2)}) copy-start(bf16[512,4096]{1,0:T(8,128)(2,1)} %param.28) | copy-start | bytes 12582916
  75.2 3.7 %copy-start.19 = (f32[512]{0:T(512)S(1)}, f32[512]{0:T(512)}, u32[]{:S(2)}) copy-start(f32[512]{0:T(512)} %param.27) | copy-start | bytes 6148
  78.9 5.4 %copy-start.3 = (bf16[1,256,768]{2,1,0:T(8,128)(2,1)S(1)}, bf16[1,256,768]{2,1,0:T(8,128)(2,1)}, u32[]{:S(2)}) copy-start(bf16[1,256,768]{2,1,0:T(8,128)(2,1)} %param.35) | copy-start | bytes 1179652
  78.9 55.0 %copy-start.17 = (s32[1,32]{1,0:T(1,128)S(1)}, s32[1,32]{1,0:T(1,128)}, u32[]{:S(2)}) copy-start(s32[1,32]{1,0:T(1,128)} %param.33) | copy-start | bytes 388
  78.9 63.5 %copy-start.13 = (s32[32,10]{0,1:T(8,128)S(1)}, s32[32,10]{0,1:T(8,128)}, u32[]{:S(2)}) copy-start(s32[32,10]{0,1:T(8,128)} %param.32) | copy-start | bytes 3844
  78.9 64.2 %copy-start.21 = (u32[256]{0:T(256)S(1)}, u32[256]{0:T(256)}, u32[]{:S(2)}) copy-start(u32[256]{0:T(256)} %constant.81) | copy-start | bytes 3076
  83.5 133.8 %copy-start.14 = (f32[4096]{0:T(1024)S(1)}, f32[4096]{0:T(1024)}, u32[]{:S(2)}) copy-start(f32[4096]{0:T(1024)} %param.30) | copy-start | bytes 49156
  83.5 174.3 %all-gather.7.cloned.1.call-start = ((), (), s32[]{:S(2)}) async-start(), calls=%async_computation.5 | async-start | bytes 13369344 | tf_op jit(solution)/shard_map/all_gather | solution.py:178
  84.2 7.2 %collective-permute-start.1 = (bf16[256,768]{1,0:T(8,128)(2,1)S(1)}, bf16[256,768]{1,0:T(8,128)(2,1)S(1)}, u32[]{:S(2)}, u32[]{:S(2)}) collective-permute-start(bf16[256,768]{1,0:T(8,128)(2,1)S(1)} %bitcast.150), channel_id=1, source_target_pairs={{0,16},{16,32},{32,48},{48,64},{64,80},{80,96},{96,112},{112,128},... | collective-permute-start | bytes 1179656 | tf_op jit(solution)/shard_map/ppermute | solution.py:31
  91.5 7.2 %collective-permute-start.2 = (bf16[256,768]{1,0:T(8,128)(2,1)S(1)}, bf16[256,768]{1,0:T(8,128)(2,1)S(1)}, u32[]{:S(2)}, u32[]{:S(2)}) collective-permute-start(bf16[256,768]{1,0:T(8,128)(2,1)S(1)} %collective-permute-done.1), channel_id=1, source_target_pairs={{0,16},{16,32},{32,48},{48,64},{64,80},{80,96},{96,112},{112,128},... | collective-permute-start | bytes 1179656 | tf_op jit(solution)/shard_map/ppermute | solution.py:31
  92.3 7.2 %collective-permute-start.9 = (bf16[256,768]{1,0:T(8,128)(2,1)S(1)}, bf16[256,768]{1,0:T(8,128)(2,1)S(1)}, u32[]{:S(2)}, u32[]{:S(2)}) collective-permute-start(bf16[256,768]{1,0:T(8,128)(2,1)S(1)} %bitcast.151), channel_id=1, source_target_pairs={{16,0},{32,16},{48,32},{64,48},{80,64},{96,80},{112,96},{128,112},... | collective-permute-start | bytes 1179656 | tf_op jit(solution)/shard_map/ppermute | solution.py:33
  98.7 26.8 %copy-start.7 = (bf16[256,768]{1,0:T(8,128)(2,1)}, bf16[256,768]{1,0:T(8,128)(2,1)S(1)}, u32[]{:S(2)}) copy-start(bf16[256,768]{1,0:T(8,128)(2,1)S(1)} %collective-permute-done.2) | copy-start | bytes 1179652
  98.7 18.4 %collective-permute-start.3 = (bf16[256,768]{1,0:T(8,128)(2,1)S(1)}, bf16[256,768]{1,0:T(8,128)(2,1)S(1)}, u32[]{:S(2)}, u32[]{:S(2)}) collective-permute-start(bf16[256,768]{1,0:T(8,128)(2,1)S(1)} %collective-permute-done.2), channel_id=1, source_target_pairs={{0,16},{16,32},{32,48},{48,64},{64,80},{80,96},{96,112},{112,128},... | collective-permute-start | bytes 1179656 | tf_op jit(solution)/shard_map/ppermute | solution.py:31
  99.5 17.5 %copy-start.5 = (bf16[256,768]{1,0:T(8,128)(2,1)}, bf16[256,768]{1,0:T(8,128)(2,1)S(1)}, u32[]{:S(2)}) copy-start(bf16[256,768]{1,0:T(8,128)(2,1)S(1)} %collective-permute-done.9) | copy-start | bytes 1179652
  99.5 17.5 %collective-permute-start.10 = (bf16[256,768]{1,0:T(8,128)(2,1)S(1)}, bf16[256,768]{1,0:T(8,128)(2,1)S(1)}, u32[]{:S(2)}, u32[]{:S(2)}) collective-permute-start(bf16[256,768]{1,0:T(8,128)(2,1)S(1)} %collective-permute-done.9), channel_id=1, source_target_pairs={{16,0},{32,16},{48,32},{64,48},{80,64},{96,80},{112,96},{128,112},... | collective-permute-start | bytes 1179656 | tf_op jit(solution)/shard_map/ppermute | solution.py:33
  117.0 16.8 %copy-start.10 = (bf16[256,768]{1,0:T(8,128)(2,1)}, bf16[256,768]{1,0:T(8,128)(2,1)S(1)}, u32[]{:S(2)}) copy-start(bf16[256,768]{1,0:T(8,128)(2,1)S(1)} %collective-permute-done.3) | copy-start | bytes 1179652
  117.0 8.4 %collective-permute-start.4 = (bf16[256,768]{1,0:T(8,128)(2,1)S(1)}, bf16[256,768]{1,0:T(8,128)(2,1)S(1)}, u32[]{:S(2)}, u32[]{:S(2)}) collective-permute-start(bf16[256,768]{1,0:T(8,128)(2,1)S(1)} %collective-permute-done.3), channel_id=1, source_target_pairs={{0,16},{16,32},{32,48},{48,64},{64,80},{80,96},{96,112},{112,128},... | collective-permute-start | bytes 1179656 | tf_op jit(solution)/shard_map/ppermute | solution.py:31
  117.1 11.5 %copy-start.8 = (bf16[256,768]{1,0:T(8,128)(2,1)}, bf16[256,768]{1,0:T(8,128)(2,1)S(1)}, u32[]{:S(2)}) copy-start(bf16[256,768]{1,0:T(8,128)(2,1)S(1)} %collective-permute-done.10) | copy-start | bytes 1179652
  117.1 8.4 %collective-permute-start.11 = (bf16[256,768]{1,0:T(8,128)(2,1)S(1)}, bf16[256,768]{1,0:T(8,128)(2,1)S(1)}, u32[]{:S(2)}, u32[]{:S(2)}) collective-permute-start(bf16[256,768]{1,0:T(8,128)(2,1)S(1)} %collective-permute-done.10), channel_id=1, source_target_pairs={{16,0},{32,16},{48,32},{64,48},{80,64},{96,80},{112,96},{128,112},... | collective-permute-start | bytes 1179656 | tf_op jit(solution)/shard_map/ppermute | solution.py:33
  125.4 8.4 %copy-start.11 = (bf16[256,768]{1,0:T(8,128)(2,1)}, bf16[256,768]{1,0:T(8,128)(2,1)S(1)}, u32[]{:S(2)}) copy-start(bf16[256,768]{1,0:T(8,128)(2,1)S(1)} %collective-permute-done.4) | copy-start | bytes 1179652
  125.4 8.4 %collective-permute-start.5 = (bf16[256,768]{1,0:T(8,128)(2,1)S(1)}, bf16[256,768]{1,0:T(8,128)(2,1)S(1)}, u32[]{:S(2)}, u32[]{:S(2)}) collective-permute-start(bf16[256,768]{1,0:T(8,128)(2,1)S(1)} %collective-permute-done.4), channel_id=1, source_target_pairs={{0,16},{16,32},{32,48},{48,64},{64,80},{80,96},{96,112},{112,128},... | collective-permute-start | bytes 1179656 | tf_op jit(solution)/shard_map/ppermute | solution.py:31
  125.5 90.5 %copy-start.4 = (bf16[256,768]{1,0:T(8,128)(2,1)}, bf16[256,768]{1,0:T(8,128)(2,1)S(1)}, u32[]{:S(2)}) copy-start(bf16[256,768]{1,0:T(8,128)(2,1)S(1)} %collective-permute-done.11) | copy-start | bytes 1179652
  125.5 8.5 %collective-permute-start.12 = (bf16[256,768]{1,0:T(8,128)(2,1)S(1)}, bf16[256,768]{1,0:T(8,128)(2,1)}, u32[]{:S(2)}, u32[]{:S(2)}) collective-permute-start(bf16[256,768]{1,0:T(8,128)(2,1)S(1)} %collective-permute-done.11), channel_id=1, source_target_pairs={{16,0},{32,16},{48,32},{64,48},{80,64},{96,80},{112,96},{128,112},... | collective-permute-start | bytes 1179656 | tf_op jit(solution)/shard_map/ppermute | solution.py:33
  133.9 0.7 copy-start.12
  133.9 8.5 %collective-permute-start.6 = (bf16[256,768]{1,0:T(8,128)(2,1)S(1)}, bf16[256,768]{1,0:T(8,128)(2,1)}, u32[]{:S(2)}, u32[]{:S(2)}) collective-permute-start(bf16[256,768]{1,0:T(8,128)(2,1)S(1)} %collective-permute-done.5), channel_id=1, source_target_pairs={{0,16},{16,32},{32,48},{48,64},{64,80},{80,96},{96,112},{112,128},... | collective-permute-start | bytes 1179656 | tf_op jit(solution)/shard_map/ppermute | solution.py:31
  134.6 9.8 %collective-permute-start.13 = (bf16[256,768]{1,0:T(8,128)(2,1)}, bf16[256,768]{1,0:T(8,128)(2,1)}, u32[]{:S(2)}, u32[]{:S(2)}) collective-permute-start(bf16[256,768]{1,0:T(8,128)(2,1)} %collective-permute-done.12), channel_id=1, source_target_pairs={{16,0},{32,16},{48,32},{64,48},{80,64},{96,80},{112,96},{128,112},... | collective-permute-start | bytes 1179656 | tf_op jit(solution)/shard_map/ppermute | solution.py:33
  142.4 8.8 %collective-permute-start.7 = (bf16[256,768]{1,0:T(8,128)(2,1)}, bf16[256,768]{1,0:T(8,128)(2,1)}, u32[]{:S(2)}, u32[]{:S(2)}) collective-permute-start(bf16[256,768]{1,0:T(8,128)(2,1)} %collective-permute-done.6), channel_id=1, source_target_pairs={{0,16},{16,32},{32,48},{48,64},{64,80},{80,96},{96,112},{112,128},... | collective-permute-start | bytes 1179656 | tf_op jit(solution)/shard_map/ppermute | solution.py:31
  144.4 28.9 %copy-start.6 = (bf16[256,768]{1,0:T(8,128)(2,1)S(1)}, bf16[256,768]{1,0:T(8,128)(2,1)}, u32[]{:S(2)}) copy-start(bf16[256,768]{1,0:T(8,128)(2,1)} %copy-done.5) | copy-start | bytes 1179652
  144.4 29.7 %copy-start.9 = (bf16[256,768]{1,0:T(8,128)(2,1)S(1)}, bf16[256,768]{1,0:T(8,128)(2,1)}, u32[]{:S(2)}) copy-start(bf16[256,768]{1,0:T(8,128)(2,1)} %copy-done.8) | copy-start | bytes 1179652
  144.4 8.6 %collective-permute-start.14 = (bf16[256,768]{1,0:T(8,128)(2,1)}, bf16[256,768]{1,0:T(8,128)(2,1)}, u32[]{:S(2)}, u32[]{:S(2)}) collective-permute-start(bf16[256,768]{1,0:T(8,128)(2,1)} %collective-permute-done.13), channel_id=1, source_target_pairs={{16,0},{32,16},{48,32},{64,48},{80,64},{96,80},{112,96},{128,112},... | collective-permute-start | bytes 1179656 | tf_op jit(solution)/shard_map/ppermute | solution.py:33
  151.1 9.1 %collective-permute-start.8 = (bf16[256,768]{1,0:T(8,128)(2,1)}, bf16[256,768]{1,0:T(8,128)(2,1)S(1)}, u32[]{:S(2)}, u32[]{:S(2)}) collective-permute-start(bf16[256,768]{1,0:T(8,128)(2,1)} %collective-permute-done.7), channel_id=1, source_target_pairs={{0,16},{16,32},{32,48},{48,64},{64,80},{80,96},{96,112},{112,128},... | collective-permute-start | bytes 1179656 | tf_op jit(solution)/shard_map/ppermute | solution.py:31
  153.0 77.3 %collective-permute-start.15 = (bf16[256,768]{1,0:T(8,128)(2,1)}, bf16[256,768]{1,0:T(8,128)(2,1)}, u32[]{:S(2)}, u32[]{:S(2)}) collective-permute-start(bf16[256,768]{1,0:T(8,128)(2,1)} %collective-permute-done.14), channel_id=1, source_target_pairs={{16,0},{32,16},{48,32},{64,48},{80,64},{96,80},{112,96},{128,112},... | collective-permute-start | bytes 1179656 | tf_op jit(solution)/shard_map/ppermute | solution.py:33
  217.3 58.5 %copy-start.1 = (f32[32,4096]{1,0:T(8,128)}, f32[32,4096]{1,0:T(8,128)S(1)}, u32[]{:S(2)}) copy-start(f32[32,4096]{1,0:T(8,128)S(1)} %get-tuple-element.83) | copy-start | bytes 1572868
  218.8 19.7 %all-to-all-start = ((bf16[16,8,4096]{2,1,0:T(8,128)(2,1)}), bf16[16,8,4096]{2,1,0:T(8,128)(2,1)}, u32[]{:S(2)}, u32[]{:S(2)}) async-start(bf16[16,8,4096]{2,1,0:T(8,128)(2,1)} %convolution_convert_fusion.3), calls=%async_computation.1 | async-start | bytes 2097152 | tf_op jit(solution)/shard_map/all_to_all | solution.py:175
  238.5 27.2 %slice-start = ((s8[6291456]{0:T(1024)(128)(4,1)}), s8[2097152]{0:T(1024)(128)(4,1)S(1)}, s32[]{:S(2)}) async-start(s8[6291456]{0:T(1024)(128)(4,1)} %bitcast.136), calls=%async_computation.6 | async-start | bytes 4194304
  257.8 8.0 %slice-start.1 = ((s8[6291456]{0:T(1024)(128)(4,1)}), s8[4194304]{0:T(1024)(128)(4,1)S(1)}, s32[]{:S(2)}) async-start(s8[6291456]{0:T(1024)(128)(4,1)} %bitcast.136), calls=%async_computation.7 | async-start | bytes 8388608
  268.9 25.0 %all-to-all-start.1 = ((bf16[16,8,4096]{2,1,0:T(8,128)(2,1)}), bf16[16,8,4096]{2,1,0:T(8,128)(2,1)S(1)}, u32[]{:S(2)}, u32[]{:S(2)}) async-start(bf16[16,8,4096]{2,1,0:T(8,128)(2,1)} %fusion), calls=%async_computation.2 | async-start | bytes 2097152 | tf_op jit(solution)/shard_map/all_to_all | solution.py:194
Sparse Core Ops, SparseCore 0:
  25.5 44.9 all-gather.4
  83.6 99.2 reduce-scatter.1
  184.8 72.9 all-gather.6
